TPU v7x, 32 devices: a whole 2x2x4 slice. The times are simulated.
32 devices in a mesh: dp: 2 (over x), context: 8 (over z, core), tensor: 2 (over y).
Axes of the slice: x: 2, y: 2, z: 4, core: 2. Of those that a mesh axis runs over, the one named last changes fastest.
Arguments:
- tokens: bfloat16 [4, 4096, 768], P('dp', 'context'), may hold values from -6 to 6
- documents: int32 [4, 4096], P('dp', 'context'), may hold values from 0 to 15, never falling along the last dimension, each value on 1 to 1024 neighbouring positions
- norm_gain: float32 [768], P(('dp', 'context')), may hold values from 0.5 to 1.5
- entry_weight: float32 [768, 2, 1536], P(('dp', 'context'), None, 'tensor'), may hold values from -0.21875 to 0.21875
- state_weight: float32 [768, 256], P(('dp', 'context')), may hold values from -0.21875 to 0.21875
- step_weight: float32 [768, 24], P(('dp', 'context'), 'tensor'), may hold values from -0.109375 to 0.109375
- inner_kernel: float32 [5, 1536], P(None, 'tensor'), may hold values from -0.5 to 0.5
- state_filter: float32 [5, 256], replicated, may hold values from -0.5 to 0.5
- step_bias: float32 [24], P('tensor'), may hold values from -7 to -3
- decay_log: float32 [24], P('tensor'), may hold values from -1 to 1.5
- skip_gain: float32 [24], P('tensor'), may hold values from 0.25 to 1
- gate_gain: float32 [1536], P('tensor'), may hold values from 0.5 to 1.5
- exit_weight: float32 [768, 1536], P(('dp', 'context'), 'tensor'), may hold values from -0.15625 to 0.15625
- cotangent: bfloat16 [4, 4096, 768], P('dp', 'context'), may hold values from -6 to 6
Outputs:
- block_out: bfloat16 [4, 4096, 768], P('dp', 'context')
- token_grad: float32 [4, 4096, 768], P('dp', 'context')
- norm_grad: float32 [768], P(('dp', 'context'))
- entry_grad: float32 [768, 2, 1536], P(('dp', 'context'), None, 'tensor')
- state_weight_gradient: float32 [768, 256], P(('dp', 'context'))
- step_weight_gradient: float32 [768, 24], P(('dp', 'context'), 'tensor')
- kernel_grad: float32 [5, 1536], P(None, 'tensor')
- filter_grad: float32 [5, 256], replicated
- bias_grad: float32 [24], P('tensor')
- decay_grad: float32 [24], P('tensor')
- skip_grad: float32 [24], P('tensor')
- gate_grad: float32 [1536], P('tensor')
- exit_weight_gradient: float32 [768, 1536], P(('dp', 'context'), 'tensor')
Inputs may be any that keep to these rules, and one draw needn't show every extreme that they name: `documents`: in each sequence the document numbers start at 0, never fall, every one of 0 to 15 occurs, each document has 1 to 1024 positions, and one has exactly 1024.
All inputs are finite; a program needn't handle non-finite values.
Results may differ from a plain program's by a relative error of at most 0.012.
The roundings to bfloat16 on the way count: a program that leaves them out, or rounds other values in their place, can miss the bound.
Values may be sent and summed in bfloat16 or wider, within the bound.
A program may use at most 256 MiB of HBM per device.

v0:
```python
import jax
import jax.numpy as jnp
from jax import lax
from jax.sharding import PartitionSpec as P

HEAD = 64
NSTATE = 128
CONV = 4
SPAN = 256
EPSILON = 1e-05
PRECISION_HIGH = lax.Precision.HIGHEST


def passed_along(x, axis, by):
    count = lax.axis_size(axis)
    pairs = [(i, i + by) for i in range(count) if 0 <= i + by < count]
    return lax.ppermute(x, axis, pairs)


def carried_in(value, axis, join, neutral, backward):
    count, mine = (lax.axis_size(axis), lax.axis_index(axis))
    pieces = jax.tree.map(lambda part: lax.all_gather(part, axis), value)
    if backward:
        pieces = jax.tree.map(lambda part: part[::-1], pieces)
        mine = count - 1 - mine
    so_far = jax.tree.map(
        lambda part, zero: jnp.full_like(part, 0) + jnp.asarray(zero, part.dtype), value, neutral
    )

    def hop(position, so_far):
        longer = join(so_far, jax.tree.map(lambda part: part[position], pieces))
        return jax.tree.map(lambda new, old: jnp.where(position < mine, new, old), longer, so_far)

    return lax.fori_loop(0, count - 1, hop, so_far)


def prepare(extended, step_unactivated, kernel, step_bias, decay_log, ids_before, documents):
    width = documents.shape[1]
    ids_extended = jnp.concatenate([ids_before, documents], axis=1)
    preact = kernel[CONV]
    for offset in range(CONV):
        match = (ids_extended[:, offset : offset + width] == documents).astype(jnp.float32)
        preact = preact + kernel[offset] * extended[:, offset : offset + width] * match[:, :, None]
    mixed = jax.nn.silu(preact)
    inner_width = mixed.shape[2] - 2 * NSTATE
    steps = jax.nn.softplus(step_unactivated + step_bias)
    return (
        mixed[:, :, :inner_width],
        mixed[:, :, inner_width : inner_width + NSTATE],
        mixed[:, :, inner_width + NSTATE :],
        -steps * jnp.exp(decay_log),
        steps,
    )


def span_summary(inner, writer, log_decay, steps, documents, before):
    seqs, width = documents.shape
    heads = steps.shape[2]
    cumulative = jnp.cumsum(log_decay, axis=1)
    final = cumulative[:, -1]
    tail = (
        (documents == documents[:, -1:]).astype(jnp.float32)[:, :, None]
        * jnp.exp(final[:, None, :] - cumulative)
        * steps
    )
    values = inner.reshape(seqs, width, heads, HEAD)
    local = jnp.einsum("suh,suhp,sun->shpn", tail, values, writer, precision=PRECISION_HIGH)
    keep = (documents[:, -1] == before).astype(jnp.float32)
    return (local, keep[:, None] * jnp.exp(final))


def span_output(inner, writer, reader, log_decay, steps, carry_in, documents, before):
    seqs, width = documents.shape
    heads = steps.shape[2]
    cumulative = jnp.cumsum(jnp.swapaxes(log_decay, 1, 2), axis=2)
    places = jnp.arange(width)
    same = (places[:, None] >= places[None, :])[None] & (
        documents[:, :, None] == documents[:, None, :]
    )
    spread = cumulative[:, :, :, None] - cumulative[:, :, None, :]
    decay = jnp.exp(jnp.where(same[:, None], spread, 0.0)) * same[:, None].astype(jnp.float32)
    scores = jnp.einsum("stn,sun->stu", reader, writer, precision=PRECISION_HIGH)
    weights = decay * scores[:, None] * jnp.swapaxes(steps, 1, 2)[:, :, None, :]
    values = inner.reshape(seqs, width, heads, HEAD)
    local = jnp.einsum("shtu,suhp->sthp", weights, values, precision=PRECISION_HIGH)
    opened = (documents == before[:, None]).astype(jnp.float32)
    carried = jnp.einsum("stn,shpn->sthp", reader, carry_in, precision=PRECISION_HIGH)
    growth = opened[:, :, None] * jnp.exp(jnp.swapaxes(cumulative, 1, 2))
    result = local + growth[:, :, :, None] * carried
    return result.reshape(seqs, width, heads * HEAD)


def span_bounds(documents, before):
    width = documents.shape[1]
    length = min(SPAN, width)
    bounds = []
    for index in range(width // length):
        first = index * length
        entry = before if index == 0 else documents[:, first - 1]
        bounds.append((first, first + length, entry))
    return bounds


def block_state(inner, writer, log_decay, steps, documents, before):
    state = None
    gain = None
    for first, last, entry in span_bounds(documents, before):
        local, factor = span_summary(
            inner[:, first:last],
            writer[:, first:last],
            log_decay[:, first:last],
            steps[:, first:last],
            documents[:, first:last],
            entry,
        )
        if state is None:
            state, gain = (local, factor)
        else:
            state = factor[:, :, None, None] * state + local
            gain = gain * factor
    return (state, gain)


def block_output(inner, writer, reader, log_decay, steps, carry_in, documents, before):
    pieces = []
    entering = carry_in
    for first, last, entry in span_bounds(documents, before):
        part_docs = documents[:, first:last]
        pieces.append(
            span_output(
                inner[:, first:last],
                writer[:, first:last],
                reader[:, first:last],
                log_decay[:, first:last],
                steps[:, first:last],
                entering,
                part_docs,
                entry,
            )
        )
        if last < documents.shape[1]:
            local, factor = span_summary(
                inner[:, first:last],
                writer[:, first:last],
                log_decay[:, first:last],
                steps[:, first:last],
                part_docs,
                entry,
            )
            entering = factor[:, :, None, None] * entering + local
    return jnp.concatenate(pieces, axis=1)


def combine(earlier, later):
    return (earlier[0] * later[0], later[0][:, :, None, None] * earlier[1] + later[1])


def body(
    tokens,
    documents,
    norm_gain,
    entry_weight,
    state_weight,
    step_weight,
    inner_kernel,
    state_filter,
    step_bias,
    decay_log,
    skip_gain,
    gate_gain,
    exit_weight,
    cotangent,
):
    position = lax.axis_index("context")
    inputs = tokens.astype(jnp.float32)
    masters = (
        norm_gain.astype(jnp.bfloat16),
        entry_weight.astype(jnp.bfloat16),
        state_weight.astype(jnp.bfloat16),
        step_weight.astype(jnp.bfloat16),
        exit_weight.astype(jnp.bfloat16),
    )
    gain_low, entry_reduced, state_low, step_reduced, exit_reduced = (
        lax.all_gather(masters[0], ("dp", "context"), axis=0, tiled=True),
        lax.all_gather(masters[1], ("dp", "context"), axis=0, tiled=True),
        lax.all_gather(masters[2], ("dp", "context"), axis=0, tiled=True),
        lax.all_gather(masters[3], ("dp", "context"), axis=0, tiled=True),
        lax.all_gather(masters[4], ("dp", "context"), axis=0, tiled=True),
    )
    scale = lax.rsqrt(jnp.mean(inputs * inputs, axis=-1, keepdims=True) + EPSILON)
    hidden_activation = (inputs * scale * gain_low.astype(jnp.float32)).astype(jnp.bfloat16)
    gate_preactivation = jnp.einsum(
        "bqm,mj->bqj", hidden_activation, entry_reduced[:, 0], preferred_element_type=jnp.float32
    )
    convolution_weight = jnp.concatenate([entry_reduced[:, 1], state_low], axis=1)
    convolution_input = jnp.einsum(
        "bqm,mj->bqj", hidden_activation, convolution_weight, preferred_element_type=jnp.float32
    ).astype(jnp.bfloat16)
    step_unactivated = jnp.einsum(
        "wje,en->wjn", hidden_activation, step_reduced, preferred_element_type=jnp.float32
    )
    edge_ids = passed_along(documents[:, -(CONV - 1) :], "context", 1)
    ids_before = jnp.where(position == 0, -1, edge_ids)
    before = ids_before[:, -1]
    edge_rows = passed_along(convolution_input[:, -(CONV - 1) :], "context", 1)
    extended = jnp.concatenate([edge_rows, convolution_input], axis=1).astype(jnp.float32)
    kernel = jnp.concatenate([inner_kernel, state_filter], axis=1)

    def prepare_local(extended, step_unactivated, kernel, step_bias, decay_log):
        return prepare(
            extended, step_unactivated, kernel, step_bias, decay_log, ids_before, documents
        )

    (inner, writer, reader, log_decay, steps), prepare_back = jax.vjp(
        prepare_local, extended, step_unactivated, kernel, step_bias, decay_log
    )

    def state_local(inner, writer, log_decay, steps):
        return block_state(inner, writer, log_decay, steps, documents, before)

    (state_here, carry_gain), state_back = jax.vjp(state_local, inner, writer, log_decay, steps)
    ones = jnp.ones_like(carry_gain)
    zeros = jnp.zeros_like(state_here)
    gain_in, carry_in = carried_in(
        (carry_gain, state_here), "context", combine, (ones, zeros), False
    )

    def output_local(inner, writer, reader, log_decay, steps, carry_in):
        return block_output(inner, writer, reader, log_decay, steps, carry_in, documents, before)

    scanned, output_back = jax.vjp(output_local, inner, writer, reader, log_decay, steps, carry_in)
    heads = steps.shape[2]
    skip_wide = jnp.repeat(skip_gain, HEAD)
    output = scanned + skip_wide * inner
    gate_act = jax.nn.silu(gate_preactivation)
    gated = output * gate_act
    square_sum = lax.psum(jnp.sum(gated * gated, axis=-1), "tensor")
    inner_total = gated.shape[-1] * lax.axis_size("tensor")
    normal = lax.rsqrt(square_sum / inner_total + EPSILON)[:, :, None]
    unit_activation = (gated * normal * gate_gain).astype(jnp.bfloat16)
    partial_value_sum = jnp.einsum(
        "yjr,pr->yjp", unit_activation, exit_reduced, preferred_element_type=jnp.float32
    )
    branch_path = lax.psum(partial_value_sum, "tensor")
    block_out = (inputs + branch_path).astype(jnp.bfloat16)
    gain_back, entry_backward, state_backward_weight, step_backward, exit_backward = (
        lax.all_gather(masters[0], ("dp", "context"), axis=0, tiled=True),
        lax.all_gather(masters[1], ("dp", "context"), axis=0, tiled=True),
        lax.all_gather(masters[2], ("dp", "context"), axis=0, tiled=True),
        lax.all_gather(masters[3], ("dp", "context"), axis=0, tiled=True),
        lax.all_gather(masters[4], ("dp", "context"), axis=0, tiled=True),
    )
    exit_weight_gradient = jnp.einsum(
        "yqr,yqj->rj", cotangent, unit_activation, preferred_element_type=jnp.float32
    )
    unit_activation_gradient = jnp.einsum(
        "bqm,mj->bqj", cotangent, exit_backward, preferred_element_type=jnp.float32
    )
    gate_grad = jnp.sum(unit_activation_gradient * gated * normal, axis=(0, 1))
    scaled = unit_activation_gradient * gate_gain
    cross = lax.psum(jnp.sum(scaled * gated, axis=-1), "tensor")[:, :, None]
    gated_grad = normal * scaled - normal * normal * normal * gated * cross / inner_total
    output_grad = gated_grad * gate_act
    sigma = jax.nn.sigmoid(gate_preactivation)
    gate_preactivation_gradient = (
        gated_grad * output * sigma * (1.0 + gate_preactivation * (1.0 - sigma))
    ).astype(jnp.bfloat16)
    seqs, width = documents.shape
    skip_grad = jnp.sum((output_grad * inner).reshape(seqs, width, heads, HEAD), axis=(0, 1, 3))
    inner_one, writer_one, reader_one, decay_one, steps_one, entering = output_back(output_grad)
    gain_out, adjoint = carried_in((carry_gain, entering), "context", combine, (ones, zeros), True)
    gain_cot = jnp.sum(adjoint * carry_in, axis=(2, 3))
    inner_two, writer_two, decay_two, steps_two = state_back((adjoint, gain_cot))
    writer_sum, reader_sum = lax.psum((writer_one + writer_two, reader_one), "tensor")
    extended_grad, step_raw_full, kernel_full, bias_grad, decay_grad = prepare_back(
        (
            inner_one + inner_two + skip_wide * output_grad,
            writer_sum,
            reader_sum,
            decay_one + decay_two,
            steps_one + steps_two,
        )
    )
    edge_grad = passed_along(extended_grad[:, : CONV - 1], "context", -1)
    conv_part = extended_grad[:, CONV - 1 :]
    conv_grad = jnp.concatenate(
        [conv_part[:, : -(CONV - 1)], conv_part[:, -(CONV - 1) :] + edge_grad], axis=1
    )
    conv_low = conv_grad.astype(jnp.bfloat16)
    step_unactivated_gradient = step_raw_full.astype(jnp.bfloat16)
    inner_width = gate_preactivation.shape[-1]
    inner_convolved = conv_low[:, :, :inner_width]
    state_convolved = conv_low[:, :, inner_width:]
    gate_row_values = jnp.einsum(
        "yqr,yqj->rj",
        hidden_activation,
        gate_preactivation_gradient,
        preferred_element_type=jnp.float32,
    )
    inner_row_values = jnp.einsum(
        "yqr,yqj->rj", hidden_activation, inner_convolved, preferred_element_type=jnp.float32
    )
    entry_grad = jnp.stack([gate_row_values, inner_row_values], axis=1)
    state_weight_gradient = jnp.einsum(
        "yqr,yqj->rj", hidden_activation, state_convolved, preferred_element_type=jnp.float32
    )
    step_weight_gradient = jnp.einsum(
        "yfm,yfc->mc",
        hidden_activation,
        step_unactivated_gradient,
        preferred_element_type=jnp.float32,
    )
    hidden_part = jnp.einsum(
        "yjr,pr->yjp",
        gate_preactivation_gradient,
        entry_backward[:, 0],
        preferred_element_type=jnp.float32,
    )
    hidden_part = hidden_part + jnp.einsum(
        "yjr,pr->yjp", inner_convolved, entry_backward[:, 1], preferred_element_type=jnp.float32
    )
    hidden_part = hidden_part + jnp.einsum(
        "imr,vr->imv", step_unactivated_gradient, step_backward, preferred_element_type=jnp.float32
    )
    hidden_grad = lax.psum(hidden_part, "tensor")
    hidden_grad = hidden_grad + jnp.einsum(
        "yjr,pr->yjp", state_convolved, state_backward_weight, preferred_element_type=jnp.float32
    )
    norm_grad = jnp.sum(hidden_grad * inputs * scale, axis=(0, 1))
    normed_grad = hidden_grad * gain_back.astype(jnp.float32)
    token_grad = (
        cotangent.astype(jnp.float32)
        + scale * normed_grad
        - scale
        * scale
        * scale
        * inputs
        * jnp.sum(normed_grad * inputs, axis=-1, keepdims=True)
        / inputs.shape[-1]
    )
    shards = (
        lax.psum_scatter(norm_grad, ("dp", "context"), scatter_dimension=0, tiled=True),
        lax.psum_scatter(entry_grad, ("dp", "context"), scatter_dimension=0, tiled=True),
        lax.psum_scatter(state_weight_gradient, ("dp", "context"), scatter_dimension=0, tiled=True),
        lax.psum_scatter(step_weight_gradient, ("dp", "context"), scatter_dimension=0, tiled=True),
        lax.psum_scatter(exit_weight_gradient, ("dp", "context"), scatter_dimension=0, tiled=True),
    )
    smalls = lax.psum(
        (
            kernel_full[:, :inner_width],
            kernel_full[:, inner_width:],
            bias_grad,
            decay_grad,
            skip_grad,
            gate_grad,
        ),
        ("dp", "context"),
    )
    return (
        block_out,
        token_grad,
        shards[0],
        shards[1],
        shards[2],
        shards[3],
        smalls[0],
        smalls[1],
        smalls[2],
        smalls[3],
        smalls[4],
        smalls[5],
        shards[4],
    )


def solution(mesh):
    in_specs = (
        P("dp", "context", None),
        P("dp", "context"),
        P(("dp", "context")),
        P(("dp", "context"), None, "tensor"),
        P(("dp", "context"), None),
        P(("dp", "context"), "tensor"),
        P(None, "tensor"),
        P(),
        P("tensor"),
        P("tensor"),
        P("tensor"),
        P("tensor"),
        P(("dp", "context"), "tensor"),
        P("dp", "context", None),
    )
    out_specs = (
        P("dp", "context", None),
        P("dp", "context", None),
        P(("dp", "context")),
        P(("dp", "context"), None, "tensor"),
        P(("dp", "context"), None),
        P(("dp", "context"), "tensor"),
        P(None, "tensor"),
        P(),
        P("tensor"),
        P("tensor"),
        P("tensor"),
        P("tensor"),
        P(("dp", "context"), "tensor"),
    )
    return jax.shard_map(body, mesh=mesh, in_specs=in_specs, out_specs=out_specs, check_vma=False)
```

profile of v0, /device:TPU:0, one launch (start us, length us, event | category | flops | bytes accessed | tf_op | source)
XLA Modules:
  0.0 956.9 jit_solution(13679648080346581622)
XLA Ops:
  16.3 34.1 %all-reduce.37 = bf16[768]{0:T(1024)(128)(2,1)S(1)} all-reduce(bf16[768]{0:T(1024)(128)(2,1)S(1)} %dynamic-update-slice), channel_id=1, replica_groups=mesh['dp'=2,'context'=8,'tensor'=2] {'dp','context'}, use_global_device_ids=true, to_apply=%add.37 | all-reduce | flops 768 | bytes 3072
  51.2 17.4 %all-gather.2 = bf16[16,48,12]{1,2,0:T(8,128)(2,1)S(1)} all-gather(bf16[1,48,12]{1,2,0:T(8,128)(2,1)S(1)} %convert_bitcast_fusion), channel_id=1, replica_groups=mesh['dp'=2,'context'=8,'tensor'=2] {'dp','context'}, dimensions={0}, use_global_device_ids=true | all-gather | bytes 19584 | tf_op jit(solution)/shard_map/all_gather | solution.py:187
  78.7 20.7 %all_gather.40 = bf16[768,256]{1,0:T(8,128)(2,1)S(1)} all-gather(bf16[48,256]{1,0:T(8,128)(2,1)S(1)} %convert_element_type.95), channel_id=1, replica_groups=mesh['dp'=2,'context'=8,'tensor'=2] {'dp','context'}, dimensions={0}, use_global_device_ids=true | all-gather | bytes 417792 | tf_op jit(solution)/shard_map/all_gather | solution.py:186
  147.7 9.9 %all_gather.42 = f32[8,2,12]{2,1,0:T(2,128)} all-gather(f32[1,2,12]{2,1,0:T(2,128)S(1)} %fusion.186), channel_id=1, replica_groups=mesh['dp'=2,'context'=8,'tensor'=2] {'context'}, dimensions={0}, use_global_device_ids=true | all-gather | bytes 864 | tf_op jit(solution)/shard_map/all_gather | solution.py:22
  165.8 32.2 %all-gather.12.cloned.1.call-done = f32[16,12,64,128]{3,2,1,0:T(8,128)} async-done(((f32[2,12,64,128]{3,2,1,0:T(8,128)}), f32[16,12,64,128]{3,2,1,0:T(8,128)}) %all-gather.12.cloned.1.call-update) | async-done | bytes 6291472 | tf_op jit(solution)/shard_map/all_gather | solution.py:22
  198.0 14.4 %while.28 = (s32[]{:T(128)}, f32[2,12,64,128]{3,2,1,0:T(8,128)S(1)}, s32[]{:T(128)}, f32[8,2,12]{2,1,0:T(2,128)}, f32[8,2,12,64,128]{4,3,2,1,0:T(8,128)}, /*index=5*/s32[]{:T(128)}, s32[]{:T(128)}) while((s32[]{:T(128)}, f32[2,12,64,128]{3,2,1,0:T(8,128)S(1)}, s32[]{:T(128)}, f32[8,2,12]{2,1,0:T(2,128)}, ...), condition=%wide.region_6.7_spmd.clone, body=%wide.region_5.6_spmd.clone.sunk | while | flops 786436 | bytes 2359697 | solution.py:34
  214.9 9.6 %bitcast_add_fusion.3 = f32[2,256,12,64]{1,3,2,0:T(8,128)} fusion(f32[2,256,12,64]{1,3,2,0:T(8,128)S(1)} %fusion.151, f32[2,256,12,64]{1,3,2,0:T(8,128)S(1)} %bitcast.305, f32[2,12,256]{2,1,0:T(8,128)S(1)} %copy-done.82, f32[2,256,256]{2,1,0:T(8,128)} %fusion.169, f32[2,256,256]{2,1,0:T(8,128)S(1)} %copy-done.57, f32[2,12,256]{2,1,0:T(8,128)S(1)} %copy-done.84, ...), kind=kOutput, calls=%fused_computation.118 | convolution fusion | flops 1216610304 | bytes 5971968 | tf_op jit(solution)/shard_map/jvp(shtu,suhp->sthp)/dot_general | solution.py:85
  230.3 8.4 bitcast_add_fusion.2
  241.9 8.3 multiply_reduce_fusion.11
  255.3 6.6 multiply_reduce_fusion.8
  266.8 8.3 multiply_reduce_fusion.9
  292.9 12.6 %fusion.23 = (f32[2,12,256]{2,1,0:T(8,128)}, f32[2,12,256]{2,1,0:T(8,128)}, f32[2,12,256]{2,1,0:T(8,128)}, f32[2,256,256]{2,1,0:T(8,128)}) fusion(f32[2,12,256]{2,1,0:T(8,128)} %copy.340, f32[2,256,256]{2,1,0:T(8,128)} %fusion.169, f32[2,256,256]{2,1,0:T(8,128)} %get-tuple-element.429, f32[2,12,256]{2,1,0:T(8,128)} %copy.338, ...), kind=kOutput, calls=%fused_computation.50 | convolution fusion | flops 1231403008 | bytes 4972544 | tf_op jit(solution)/shard_map/transpose(jvp(shtu,suhp->sthp))/dot_general | solution.py:85
  310.3 8.3 fusion.13
  345.1 13.2 %fusion.21 = (f32[2,12,256]{2,1,0:T(8,128)}, f32[2,12,256]{2,1,0:T(8,128)}, f32[2,12,256]{2,1,0:T(8,128)}, f32[2,256,256]{2,1,0:T(8,128)}) fusion(f32[2,12,256]{2,1,0:T(8,128)} %copy.355, f32[2,256,256]{2,1,0:T(8,128)} %fusion.159, f32[2,256,256]{2,1,0:T(8,128)} %get-tuple-element.432, f32[2,12,256]{2,1,0:T(8,128)} %copy.353, ...), kind=kOutput, calls=%fused_computation.48 | convolution fusion | flops 1231403008 | bytes 4972544 | tf_op jit(solution)/shard_map/transpose(jvp(shtu,suhp->sthp))/dot_general | solution.py:85
  379.7 8.5 fusion.6
  425.1 14.0 %while.29 = (s32[]{:T(128)}, f32[2,12,64,128]{3,2,1,0:T(8,128)S(1)}, s32[]{:T(128)}, f32[8,2,12]{2,1,0:T(2,128)}, f32[8,2,12,64,128]{4,3,2,1,0:T(8,128)}, /*index=5*/s32[]{:T(128)}, s32[]{:T(128)}) while((s32[]{:T(128)}, f32[2,12,64,128]{3,2,1,0:T(8,128)S(1)}, s32[]{:T(128)}, f32[8,2,12]{2,1,0:T(2,128)}, ...), condition=%wide.region_16.17_spmd.clone, body=%wide.region_15.16_spmd.clone.sunk | while | flops 786436 | bytes 2359697 | solution.py:34
  514.1 14.7 %all-reduce.47.cloned.1.call-done = (f32[2,512,128]{2,1,0:T(8,128)}, f32[2,512,128]{2,1,0:T(8,128)}) async-done(((f32[2,512,128]{2,1,0:T(8,128)}, f32[2,512,128]{2,1,0:T(8,128)}), (f32[2,512,128]{2,1,0:T(8,128)}, f32[2,512,128]{2,1,0:T(8,128)})) %all-reduce.47.cloned.1.call-update) | async-done | bytes 1048592 | tf_op jit(solution)/shard_map/psum | solution.py:274
  528.9 11.9 %multiply_reduce_fusion.7 = (f32[1024]{0:T(1024)S(1)}, f32[1024]{0:T(1024)S(1)}, f32[1024]{0:T(1024)S(1)}, f32[1024]{0:T(1024)S(1)}, f32[1024]{0:T(1024)S(1)}, /*index=5*/f32[2,512,1024]{2,1,0:T(8,128)S(1)}) fusion(f32[2,515,1024]{2,1,0:T(8,128)} %copy-done, f32[2,512]{1,0:T(2,128)S(1)} %get-tuple-element.440, f32[2,512]{1,0:T(2,128)S(1)} %get-tuple-element.441, ...), kind=kLoop, calls=%fused_computation.40 | loop fusion | flops 24112128 | bytes 29392896 | tf_op jit(solution)/shard_map/transpose(jvp())/reduce_sum | solution.py:43
  579.0 9.2 reduce-scatter.13.cloned.1.call-done
  593.1 150.2 %all-reduce.45.cloned.1.call-done = (f32[2,512,768]{2,1,0:T(8,128)}, f32[2,512,768]{2,1,0:T(8,128)}) async-done(((f32[2,512,768]{2,1,0:T(8,128)}, f32[2,512,768]{2,1,0:T(8,128)}), (f32[2,512,768]{2,1,0:T(8,128)}, f32[2,512,768]{2,1,0:T(8,128)})) %all-reduce.45.cloned.1.call-update) | async-done | bytes 6291472 | tf_op jit(solution)/shard_map/psum | solution.py:244
  749.3 63.3 %all-reduce.39 = (f32[768]{0:T(1024)S(1)}, f32[5,768]{1,0:T(8,128)}, f32[5,256]{1,0:T(8,128)}, f32[12]{0:T(128)}, f32[12]{0:T(128)}, /*index=5*/f32[12]{0:T(128)}, f32[768]{0:T(1024)}) all-reduce(f32[768]{0:T(1024)S(1)} %get-tuple-element.400, ...), channel_id=4, replica_groups=mesh['dp'=2,'context'=8,'tensor'=2] {'dp','context'}, use_global_device_ids=true, to_apply=%region_45.46.clone | all-reduce | flops 6692 | bytes 53536
  813.2 7.0 fusion.30
  825.5 64.4 %reduce-scatter.15.cloned.1.call-done = f32[48,768]{1,0:T(8,128)} async-done(((f32[768,768]{1,0:T(8,128)}), f32[48,768]{1,0:T(8,128)}) %reduce-scatter.15.cloned.1.call-update) | async-done | bytes 147472
  889.9 60.0 %reduce-scatter.11.cloned.1.call-done = f32[48,256]{1,0:T(8,128)} async-done(((f32[768,256]{1,0:T(8,128)}), f32[48,256]{1,0:T(8,128)}) %reduce-scatter.11.cloned.1.call-update) | async-done | bytes 49168 | tf_op jit(solution)/shard_map/reduce_scatter | solution.py:344
  (496 shorter events, 360.0 us)
Async XLA Ops:
  7.2 66.3 %copy-start.112 = (f32[12]{0:T(128)S(1)}, f32[12]{0:T(128)}, u32[]{:S(2)}) copy-start(f32[12]{0:T(128)} %param.26) | copy-start | bytes 148
  7.2 100.6 %all-gather.8.cloned.1.call-start = ((), (), s32[]{:S(2)}) async-start(), calls=%async_computation.4 | async-start | bytes 2506752 | tf_op jit(solution)/shard_map/all_gather | solution.py:185
  8.0 93.2 %collective-permute-start.1 = (s32[2,3]{1,0:T(2,128)S(1)}, s32[2,3]{1,0:T(2,128)S(1)}, u32[]{:S(2)}, u32[]{:S(2)}) collective-permute-start(s32[2,3]{1,0:T(2,128)S(1)} %slice.211), channel_id=1, source_target_pairs={{0,2},{2,4},{4,6},{6,8},{8,10},{10,12},{12,14},{1,3},{3,5},{5,7},{... | collective-permute-start | bytes 80 | tf_op jit(solution)/shard_map/ppermute | solution.py:17
  12.0 186.0 %all-gather.12.cloned.1.call-start = ((), (), s32[]{:S(2)}) async-start(), calls=%async_computation.8 | async-start | bytes 7077888 | tf_op jit(solution)/shard_map/all_gather | solution.py:22
  13.4 61.3 %copy-start.114 = (f32[12]{0:T(128)}, f32[12]{0:T(128)S(1)}, u32[]{:S(2)}) copy-start(f32[12]{0:T(128)S(1)} %exp.91) | copy-start | bytes 148
  74.8 33.0 %copy-start.20 = (f32[2,512,12]{2,0,1:T(2,128)}, f32[2,512,12]{2,0,1:T(2,128)S(1)}, u32[]{:S(2)}) copy-start(f32[2,512,12]{2,0,1:T(2,128)S(1)} %get-tuple-element.388) | copy-start | bytes 147460
  78.4 36.0 %copy-start.34 = (f32[2,12,256]{1,0,2:T(2,128)}, f32[2,12,256]{1,0,2:T(2,128)S(1)}, u32[]{:S(2)}) copy-start(f32[2,12,256]{1,0,2:T(2,128)S(1)} %copy.347) | copy-start | bytes 73732
  111.9 4.7 collective-permute-start
  135.6 24.4 %copy-start.49 = (f32[2,256,12]{2,0,1:T(2,128)S(1)}, f32[2,256,12]{2,0,1:T(2,128)}, u32[]{:S(2)}) copy-start(f32[2,256,12]{2,0,1:T(2,128)} %get-tuple-element.426) | copy-start | bytes 73732
  135.6 24.5 %copy-start.48 = (f32[2,256,12]{2,0,1:T(2,128)S(1)}, f32[2,256,12]{2,0,1:T(2,128)}, u32[]{:S(2)}) copy-start(f32[2,256,12]{2,0,1:T(2,128)} %get-tuple-element.427) | copy-start | bytes 73732
  135.7 119.6 %all-gather.10.cloned.1.call-start = ((), (), s32[]{:S(2)}) async-start(), calls=%async_computation.5 | async-start | bytes 1253376 | tf_op jit(solution)/shard_map/all_gather | solution.py:188
  137.4 281.2 %all-gather.14.cloned.1.call-start = ((), (), s32[]{:S(2)}) async-start(), calls=%async_computation.9 | async-start | bytes 7077888 | tf_op jit(solution)/shard_map/all_gather | solution.py:22
  143.5 98.4 %copy-start.78 = (f32[768]{0:T(1024)}, f32[768]{0:T(1024)S(1)}, u32[]{:S(2)}) copy-start(f32[768]{0:T(1024)S(1)} %mul.876) | copy-start | bytes 9220
  160.2 54.7 %copy-start.60 = (f32[2,256,12]{1,2,0:T(8,128)}, f32[2,256,12]{1,2,0:T(8,128)S(1)}, u32[]{:S(2)}) copy-start(f32[2,256,12]{1,2,0:T(8,128)S(1)} %copy.343) | copy-start | bytes 73732
  291.3 237.6 %all-reduce.47.cloned.1.call-start = ((), (), s32[]{:S(2)}) async-start(), calls=%async_computation.13 | async-start | bytes 2097152 | tf_op jit(solution)/shard_map/psum | solution.py:274
  489.8 98.4 %reduce-scatter.13.cloned.1.call-start = ((), (), s32[]{:S(2)}) async-start(), calls=%async_computation.10 | async-start | bytes 417792
  508.4 235.0 %all-reduce.45.cloned.1.call-start = ((), (), s32[]{:S(2)}) async-start(), calls=%async_computation.12 | async-start | bytes 12582912 | tf_op jit(solution)/shard_map/psum | solution.py:244
  544.2 9.4 collective-permute-start.2
  561.1 262.5 %reduce-scatter.9.cloned.1.call-start = ((), (), s32[]{:S(2)}) async-start(), calls=%async_computation.6 | async-start | bytes 5013504 | tf_op jit(solution)/shard_map/reduce_scatter | solution.py:343
  568.9 320.9 %reduce-scatter.15.cloned.1.call-start = ((), (), s32[]{:S(2)}) async-start(), calls=%async_computation.11 | async-start | bytes 2506752
  578.1 371.8 %reduce-scatter.11.cloned.1.call-start = ((), (), s32[]{:S(2)}) async-start(), calls=%async_computation.7 | async-start | bytes 835584 | tf_op jit(solution)/shard_map/reduce_scatter | solution.py:344
  589.8 153.6 %copy-start.31 = (bf16[2,512,768]{2,1,0:T(8,128)(2,1)S(1)}, bf16[2,512,768]{2,1,0:T(8,128)(2,1)}, u32[]{:S(2)}) copy-start(bf16[2,512,768]{2,1,0:T(8,128)(2,1)} %param.18) | copy-start | bytes 4718596
  589.8 153.6 %copy-start.43 = (bf16[768,256]{1,0:T(8,128)(2,1)S(1)}, bf16[768,256]{1,0:T(8,128)(2,1)}, u32[]{:S(2)}) copy-start(bf16[768,256]{1,0:T(8,128)(2,1)} %copy-done.42) | copy-start | bytes 1179652
  743.4 69.8 %copy-start.107 = (f32[2,512]{1,0:T(2,128)S(1)}, f32[2,512]{1,0:T(2,128)}, u32[]{:S(2)}) copy-start(f32[2,512]{1,0:T(2,128)} %get-tuple-element.444) | copy-start | bytes 12292
  (107 other events, 639.3 us)
Sparse Core Ops, SparseCore 0:
  12.1 45.0 all-gather.7
  135.8 62.1 all-gather.11
  200.3 37.0 all-gather.9
  291.4 63.4 all-gather.13
  490.0 38.8 all-reduce.46
  532.6 55.5 reduce-scatter.12
  590.7 152.5 all-reduce.44
  747.7 75.8 reduce-scatter.8
  827.9 61.9 reduce-scatter.14
  894.3 55.5 reduce-scatter.10
where the time goes:
time: 967 us; the launch traced here: 957 us
  waiting for transfers between devices  334 us (35%)
  matrix products  177 us (18%)
  blocking collectives  155 us (16%)
  other arithmetic  143 us (15%)
  local copies, waits for them, and re-layouts  122 us (13%)
  between operations  17.2 us (2%)
    psum x1, waiting for transfers between devices, body(): branch_path = lax.psum(partial_value_sum, 'tensor')  150 us
    unnamed x2, blocking collectives  97.4 us
    unnamed x12, waiting for transfers between devices  73.8 us
    dot_general x6, matrix products, span_output(): jnp.einsum('shtu,suhp->sthp', weights, values, precision=PRECISION_HIGH)  60.7 us
    reduce_scatter x1, waiting for transfers between devices, body(): lax.psum_scatter(state_weight_gradient, ('dp', 'context'), scatter_dimens...  60 us
    another operation x22, other arithmetic  36.2 us
    all_gather x2, waiting for transfers between devices, carried_in(): pieces = jax.tree.map(lambda part: lax.all_gather(part, axis), value)  32.2 us
    dot_general x8, matrix products, span_summary(): jnp.einsum('suh,suhp,sun->shpn', tail, values, writer, precision=PRECISIO...  29.6 us
  transfers between devices with their start and end apart: 13, of which 7 were waited for; matrix products, arithmetic and copies ran while one was open for 32% of the time, Pallas kernels for 0%

commit v1 on v0

--- a/solution.py
+++ b/solution.py
@@ -241,7 +241,7 @@
     partial_value_sum = jnp.einsum(
         "yjr,pr->yjp", unit_activation, exit_reduced, preferred_element_type=jnp.float32
     )
-    branch_path = lax.psum(partial_value_sum, "tensor")
+    branch_path = jnp.sum(lax.all_gather(partial_value_sum, "tensor"), axis=0)
     block_out = (inputs + branch_path).astype(jnp.bfloat16)
     gain_back, entry_backward, state_backward_weight, step_backward, exit_backward = (
         lax.all_gather(masters[0], ("dp", "context"), axis=0, tiled=True),

time: 967 us -> 879 us (0.909)
  waiting for transfers between devices: 334 us -> 238 us
    psum x1, waiting for transfers between devices: 150 us -> 71.4 us  [body(): hidden_grad = lax.psum(hidden_part, 'tensor')]
    psum x1, waiting for transfers between devices: 14.7 us -> 0.01 us  [body(): lax.psum((writer_one + writer_two, reader_one), 'tensor')]
    unnamed x12 -> x13, waiting for transfers between devices: 73.8 us -> 64.4 us
    unnamed x244 -> x270, local copies, waits for them, and re-layouts: 20.9 us -> 21.8 us
  transfers between devices with their start and end apart: 13 -> 14, of which waited for: 7 -> 6; matrix products, arithmetic and copies ran while one was open for 32% -> 41% of each run, Pallas kernels for 0% -> 0%
where the time goes in v1:
time: 879 us; the launch traced here: 869 us
  waiting for transfers between devices  238 us (27%)
  matrix products  178 us (20%)
  blocking collectives  156 us (18%)
  other arithmetic  149 us (17%)
  local copies, waits for them, and re-layouts  122 us (14%)
  between operations  17.1 us (2%)
    unnamed x2, blocking collectives  97.8 us
    psum x1, waiting for transfers between devices, body(): hidden_grad = lax.psum(hidden_part, 'tensor')  71.4 us
    unnamed x13, waiting for transfers between devices  64.4 us
    reduce_scatter x1, waiting for transfers between devices, body(): lax.psum_scatter(state_weight_gradient, ('dp', 'context'), scatter_dimens...  60.1 us
    dot_general x6, matrix products, span_output(): jnp.einsum('shtu,suhp->sthp', weights, values, precision=PRECISION_HIGH)  58.7 us
    all_gather x2, waiting for transfers between devices, carried_in(): pieces = jax.tree.map(lambda part: lax.all_gather(part, axis), value)  39.8 us
    another operation x22, other arithmetic  35.2 us
    dot_general x8, matrix products, span_summary(): jnp.einsum('suh,suhp,sun->shpn', tail, values, writer, precision=PRECISIO...  28.1 us
  transfers between devices with their start and end apart: 14, of which 6 were waited for; matrix products, arithmetic and copies ran while one was open for 41% of the time, Pallas kernels for 0%

profile of v1, /device:TPU:0, one launch (start us, length us, event | category | flops | bytes accessed | tf_op | source)
XLA Modules:
  0.0 868.9 jit_solution(17238468746078848659)
XLA Ops:
  16.3 34.1 %all-reduce.37 = bf16[768]{0:T(1024)(128)(2,1)S(1)} all-reduce(bf16[768]{0:T(1024)(128)(2,1)S(1)} %dynamic-update-slice), channel_id=1, replica_groups=mesh['dp'=2,'context'=8,'tensor'=2] {'dp','context'}, use_global_device_ids=true, to_apply=%add.37 | all-reduce | flops 768 | bytes 3072
  51.2 17.4 %all-gather.3 = bf16[16,48,12]{1,2,0:T(8,128)(2,1)S(1)} all-gather(bf16[1,48,12]{1,2,0:T(8,128)(2,1)S(1)} %convert_bitcast_fusion), channel_id=1, replica_groups=mesh['dp'=2,'context'=8,'tensor'=2] {'dp','context'}, dimensions={0}, use_global_device_ids=true | all-gather | bytes 19584 | tf_op jit(solution)/shard_map/all_gather | solution.py:187
  78.7 20.7 %all_gather.46 = bf16[768,256]{1,0:T(8,128)(2,1)S(1)} all-gather(bf16[48,256]{1,0:T(8,128)(2,1)S(1)} %convert_element_type.95), channel_id=1, replica_groups=mesh['dp'=2,'context'=8,'tensor'=2] {'dp','context'}, dimensions={0}, use_global_device_ids=true | all-gather | bytes 417792 | tf_op jit(solution)/shard_map/all_gather | solution.py:186
  147.7 9.9 %all_gather.48 = f32[8,2,12]{2,1,0:T(2,128)} all-gather(f32[1,2,12]{2,1,0:T(2,128)S(1)} %fusion.186), channel_id=1, replica_groups=mesh['dp'=2,'context'=8,'tensor'=2] {'context'}, dimensions={0}, use_global_device_ids=true | all-gather | bytes 864 | tf_op jit(solution)/shard_map/all_gather | solution.py:22
  165.7 32.1 %all-gather.14.cloned.1.call-done = f32[16,12,64,128]{3,2,1,0:T(8,128)} async-done(((f32[2,12,64,128]{3,2,1,0:T(8,128)}), f32[16,12,64,128]{3,2,1,0:T(8,128)}) %all-gather.14.cloned.1.call-update) | async-done | bytes 6291472 | tf_op jit(solution)/shard_map/all_gather | solution.py:22
  197.9 14.4 %while.28 = (s32[]{:T(128)}, f32[2,12,64,128]{3,2,1,0:T(8,128)S(1)}, s32[]{:T(128)}, f32[8,2,12]{2,1,0:T(2,128)}, f32[8,2,12,64,128]{4,3,2,1,0:T(8,128)}, /*index=5*/s32[]{:T(128)}, s32[]{:T(128)}) while((s32[]{:T(128)}, f32[2,12,64,128]{3,2,1,0:T(8,128)S(1)}, s32[]{:T(128)}, f32[8,2,12]{2,1,0:T(2,128)}, ...), condition=%wide.region_6.7_spmd.clone, body=%wide.region_5.6_spmd.clone.sunk | while | flops 786436 | bytes 2359697 | solution.py:34
  214.7 9.6 %bitcast_add_fusion.3 = f32[2,256,12,64]{1,3,2,0:T(8,128)} fusion(f32[2,256,12,64]{1,3,2,0:T(8,128)S(1)} %fusion.151, f32[2,256,12,64]{1,3,2,0:T(8,128)S(1)} %bitcast.306, f32[2,12,256]{2,1,0:T(8,128)S(1)} %copy-done.97, f32[2,256,256]{2,1,0:T(8,128)} %fusion.169, f32[2,256,256]{2,1,0:T(8,128)S(1)} %copy-done.62, f32[2,12,256]{2,1,0:T(8,128)S(1)} %copy-done.100, ...), kind=kOutput, calls=%fused_computation.118 | convolution fusion | flops 1216610304 | bytes 5971968 | tf_op jit(solution)/shard_map/jvp(shtu,suhp->sthp)/dot_general | solution.py:85
  230.2 8.4 bitcast_add_fusion.2
  241.7 8.3 multiply_reduce_fusion.11
  255.2 6.6 multiply_reduce_fusion.8
  266.7 8.3 multiply_reduce_fusion.9
  292.6 12.6 %fusion.23 = (f32[2,12,256]{2,1,0:T(8,128)}, f32[2,12,256]{2,1,0:T(8,128)}, f32[2,12,256]{2,1,0:T(8,128)}, f32[2,256,256]{2,1,0:T(8,128)}) fusion(f32[2,12,256]{2,1,0:T(8,128)} %copy.340, f32[2,256,256]{2,1,0:T(8,128)} %fusion.169, f32[2,256,256]{2,1,0:T(8,128)} %get-tuple-element.427, f32[2,12,256]{2,1,0:T(8,128)} %copy.338, ...), kind=kOutput, calls=%fused_computation.50 | convolution fusion | flops 1231403008 | bytes 4972544 | tf_op jit(solution)/shard_map/transpose(jvp(shtu,suhp->sthp))/dot_general | solution.py:85
  324.1 11.6 %fusion.21 = (f32[2,12,256]{2,1,0:T(8,128)}, f32[2,12,256]{2,1,0:T(8,128)}, f32[2,12,256]{2,1,0:T(8,128)}, f32[2,256,256]{2,1,0:T(8,128)S(1)}) fusion(f32[2,12,256]{2,1,0:T(8,128)S(1)} %copy-done.96, f32[2,256,256]{2,1,0:T(8,128)S(1)} %copy-done.61, f32[2,256,256]{2,1,0:T(8,128)S(1)} %copy-done.59, f32[2,12,256]{2,1,0:T(8,128)S(1)} %copy-done.99, ...), kind=kOutput, calls=%fused_computation.48 | convolution fusion | flops 1231403008 | bytes 4972544 | tf_op jit(solution)/shard_map/transpose(jvp(shtu,suhp->sthp))/dot_general | solution.py:85
  346.9 7.7 all-gather.18.cloned.1.call-done
  354.6 6.6 rev.7
  361.1 14.2 %while.29 = (s32[]{:T(128)}, f32[2,12,64,128]{3,2,1,0:T(8,128)S(1)}, s32[]{:T(128)}, f32[8,2,12]{2,1,0:T(2,128)}, f32[8,2,12,64,128]{4,3,2,1,0:T(8,128)}, /*index=5*/s32[]{:T(128)}, s32[]{:T(128)}) while((s32[]{:T(128)}, f32[2,12,64,128]{3,2,1,0:T(8,128)S(1)}, s32[]{:T(128)}, f32[8,2,12]{2,1,0:T(2,128)}, ...), condition=%wide.region_16.17_spmd.clone, body=%wide.region_15.16_spmd.clone.sunk | while | flops 786436 | bytes 2359697 | solution.py:34
  398.9 8.3 fusion.13
  439.1 8.2 fusion.6
  519.7 11.9 %multiply_reduce_fusion.7 = (f32[1024]{0:T(1024)S(1)}, f32[1024]{0:T(1024)S(1)}, f32[1024]{0:T(1024)S(1)}, f32[1024]{0:T(1024)S(1)}, f32[1024]{0:T(1024)S(1)}, /*index=5*/f32[2,512,1024]{2,1,0:T(8,128)S(1)}) fusion(f32[2,515,1024]{2,1,0:T(8,128)} %copy-done, f32[2,512]{1,0:T(2,128)S(1)} %get-tuple-element.438, f32[2,512]{1,0:T(2,128)S(1)} %get-tuple-element.439, ...), kind=kLoop, calls=%fused_computation.40 | loop fusion | flops 24112128 | bytes 29392896 | tf_op jit(solution)/shard_map/transpose(jvp())/reduce_sum | solution.py:43
  584.1 71.4 %all-reduce.44.cloned.1.call-done = f32[2,512,768]{2,1,0:T(8,128)} async-done(((f32[2,512,768]{2,1,0:T(8,128)}), f32[2,512,768]{2,1,0:T(8,128)}) %all-reduce.44.cloned.1.call-update) | async-done | bytes 3145744 | tf_op jit(solution)/shard_map/psum | solution.py:325
  661.1 63.7 %all-reduce.39 = (f32[768]{0:T(1024)S(1)}, f32[5,768]{1,0:T(8,128)}, f32[5,256]{1,0:T(8,128)}, f32[12]{0:T(128)}, f32[12]{0:T(128)}, /*index=5*/f32[12]{0:T(128)}, f32[768]{0:T(1024)}) all-reduce(f32[768]{0:T(1024)S(1)} %get-tuple-element.398, ...), channel_id=5, replica_groups=mesh['dp'=2,'context'=8,'tensor'=2] {'dp','context'}, use_global_device_ids=true, to_apply=%region_45.46.clone | all-reduce | flops 6692 | bytes 53536
  725.3 7.9 fusion.30
  737.7 64.2 %reduce-scatter.15.cloned.1.call-done = f32[48,768]{1,0:T(8,128)} async-done(((f32[768,768]{1,0:T(8,128)}), f32[48,768]{1,0:T(8,128)}) %reduce-scatter.15.cloned.1.call-update) | async-done | bytes 147472
  802.0 60.1 %reduce-scatter.11.cloned.1.call-done = f32[48,256]{1,0:T(8,128)} async-done(((f32[768,256]{1,0:T(8,128)}), f32[48,256]{1,0:T(8,128)}) %reduce-scatter.11.cloned.1.call-update) | async-done | bytes 49168 | tf_op jit(solution)/shard_map/reduce_scatter | solution.py:344
  (525 shorter events, 361.1 us)
Async XLA Ops:
  7.2 66.3 %copy-start.125 = (f32[12]{0:T(128)S(1)}, f32[12]{0:T(128)}, u32[]{:S(2)}) copy-start(f32[12]{0:T(128)} %param.26) | copy-start | bytes 148
  7.2 100.5 %all-gather.10.cloned.1.call-start = ((), (), s32[]{:S(2)}) async-start(), calls=%async_computation.4 | async-start | bytes 2506752 | tf_op jit(solution)/shard_map/all_gather | solution.py:185
  8.0 93.1 %collective-permute-start.1 = (s32[2,3]{1,0:T(2,128)S(1)}, s32[2,3]{1,0:T(2,128)S(1)}, u32[]{:S(2)}, u32[]{:S(2)}) collective-permute-start(s32[2,3]{1,0:T(2,128)S(1)} %slice.211), channel_id=1, source_target_pairs={{0,2},{2,4},{4,6},{6,8},{8,10},{10,12},{12,14},{1,3},{3,5},{5,7},{... | collective-permute-start | bytes 80 | tf_op jit(solution)/shard_map/ppermute | solution.py:17
  12.0 185.9 %all-gather.14.cloned.1.call-start = ((), (), s32[]{:S(2)}) async-start(), calls=%async_computation.9 | async-start | bytes 7077888 | tf_op jit(solution)/shard_map/all_gather | solution.py:22
  13.4 61.3 %copy-start.127 = (f32[12]{0:T(128)}, f32[12]{0:T(128)S(1)}, u32[]{:S(2)}) copy-start(f32[12]{0:T(128)S(1)} %exp.91) | copy-start | bytes 148
  111.7 4.7 collective-permute-start
  135.6 119.5 %all-gather.12.cloned.1.call-start = ((), (), s32[]{:S(2)}) async-start(), calls=%async_computation.5 | async-start | bytes 1253376 | tf_op jit(solution)/shard_map/all_gather | solution.py:188
  137.3 217.3 %all-gather.18.cloned.1.call-start = ((), (), s32[]{:S(2)}) async-start(), calls=%async_computation.11 | async-start | bytes 7077888 | tf_op jit(solution)/shard_map/all_gather | solution.py:22
  143.4 98.3 %copy-start.92 = (f32[768]{0:T(1024)}, f32[768]{0:T(1024)S(1)}, u32[]{:S(2)}) copy-start(f32[768]{0:T(1024)S(1)} %mul.876) | copy-start | bytes 9220
  160.1 54.6 %copy-start.63 = (f32[2,256,12]{1,2,0:T(8,128)}, f32[2,256,12]{1,2,0:T(8,128)S(1)}, u32[]{:S(2)}) copy-start(f32[2,256,12]{1,2,0:T(8,128)S(1)} %copy.343) | copy-start | bytes 73732
  255.1 138.4 %copy-start.90 = (f32[2,512]{1,0:T(2,128)}, f32[2,512]{1,0:T(2,128)S(1)}, u32[]{:S(2)}) copy-start(f32[2,512]{1,0:T(2,128)S(1)} %get-tuple-element.445) | copy-start | bytes 12292
  291.0 228.7 %all-reduce.46.cloned.1.call-start = ((), (), s32[]{:S(2)}) async-start(), calls=%async_computation.14 | async-start | bytes 2097152 | tf_op jit(solution)/shard_map/psum | solution.py:274
  383.4 187.0 %all-gather.16.cloned.1.call-start = ((), (), s32[]{:S(2)}) async-start(), calls=%async_computation.10 | async-start | bytes 9437184 | tf_op jit(solution)/shard_map/all_gather | solution.py:244
  407.3 169.2 %reduce-scatter.13.cloned.1.call-start = ((), (), s32[]{:S(2)}) async-start(), calls=%async_computation.12 | async-start | bytes 417792
  513.9 141.6 %all-reduce.44.cloned.1.call-start = ((), (), s32[]{:S(2)}) async-start(), calls=%async_computation.6 | async-start | bytes 6291456 | tf_op jit(solution)/shard_map/psum | solution.py:325
  531.6 46.3 %copy-start.83 = (f32[1024]{0:T(1024)}, f32[1024]{0:T(1024)S(1)}, u32[]{:S(2)}) copy-start(f32[1024]{0:T(1024)S(1)} %get-tuple-element.318) | copy-start | bytes 12292
  535.2 9.4 %collective-permute-start.2 = (f32[2,3,1024]{2,1,0:T(4,128)S(1)}, f32[2,3,1024]{2,1,0:T(4,128)S(1)}, u32[]{:S(2)}, u32[]{:S(2)}) collective-permute-start(f32[2,3,1024]{2,1,0:T(4,128)S(1)} %pad_add_fusion.5), channel_id=1, source_target_pairs={{2,0},{4,2},{6,4},{8,6},{10,8},{12,10},{14,12},{3,1},{5,3},{7,5},{... | collective-permute-start | bytes 73736 | tf_op jit(solution)/shard_map/ppermute | solution.py:17
  552.0 183.8 %reduce-scatter.9.cloned.1.call-start = ((), (), s32[]{:S(2)}) async-start(), calls=%async_computation.7 | async-start | bytes 5013504 | tf_op jit(solution)/shard_map/reduce_scatter | solution.py:343
  559.9 242.1 %reduce-scatter.15.cloned.1.call-start = ((), (), s32[]{:S(2)}) async-start(), calls=%async_computation.13 | async-start | bytes 2506752
  569.0 293.0 %reduce-scatter.11.cloned.1.call-start = ((), (), s32[]{:S(2)}) async-start(), calls=%async_computation.8 | async-start | bytes 835584 | tf_op jit(solution)/shard_map/reduce_scatter | solution.py:344
  579.5 76.0 %copy-start.24 = (f32[2,512,768]{2,1,0:T(8,128)S(1)}, f32[2,512,768]{2,1,0:T(8,128)}, u32[]{:S(2)}) copy-start(f32[2,512,768]{2,1,0:T(8,128)} %reduce_sum.296) | copy-start | bytes 9437188
  579.5 76.0 %copy-start.41 = (bf16[768,256]{1,0:T(8,128)(2,1)S(1)}, bf16[768,256]{1,0:T(8,128)(2,1)}, u32[]{:S(2)}) copy-start(bf16[768,256]{1,0:T(8,128)(2,1)} %copy-done.40) | copy-start | bytes 1179652
  584.1 77.0 %copy-start.101 = (f32[5,256]{1,0:T(8,128)S(1)}, f32[5,256]{1,0:T(8,128)}, u32[]{:S(2)}) copy-start(f32[5,256]{1,0:T(8,128)} %pad_add_fusion.7) | copy-start | bytes 15364
  584.1 141.2 %copy-start.112 = (f32[2,512]{1,0:T(2,128)S(1)}, f32[2,512]{1,0:T(2,128)}, u32[]{:S(2)}) copy-start(f32[2,512]{1,0:T(2,128)} %copy-done.109) | copy-start | bytes 12292
  (120 other events, 1024.1 us)
Sparse Core Ops, SparseCore 0:
  12.1 45.0 all-gather.9
  135.8 62.0 all-gather.13
  200.2 37.0 all-gather.11
  291.1 63.4 all-gather.17
  383.5 38.8 all-reduce.45
  423.9 80.3 all-gather.15
  514.0 54.2 reduce-scatter.12
  570.6 84.7 all-reduce.43
  659.8 75.9 reduce-scatter.8
  740.0 61.9 reduce-scatter.14
  806.5 55.5 reduce-scatter.10
